TPU v7x, 32 devices: a whole 2x2x4 slice. The times are simulated.
32 devices in a mesh: segment: 2 (over core), gx: 2 (over x), gy: 4 (over z), gz: 2 (over y).
Axes of the slice: x: 2, y: 2, z: 4, core: 2. Of those that a mesh axis runs over, the one named last changes fastest.
Arguments:
- features: bfloat16 [2, 16, 8, 128, 256], P(None, None, 'gx', 'gy', 'gz'), may hold values from -6 to 6
- weights: bfloat16 [2, 2, 16, 16, 3, 3, 3], P('segment'), may hold values from -0.4375 to 0.4375
- biases: bfloat16 [2, 2, 16], P('segment'), may hold values from -3 to 3
Outputs:
- section_out: bfloat16 [2, 2, 16, 8, 128, 256], P('segment', None, None, 'gx', 'gy', 'gz')
All inputs are finite; a program needn't handle non-finite values.
Results may differ from a plain program's by a relative error of at most 0.0054.
Values may be sent and summed in bfloat16 or wider, within the bound.
No kernel may reach another device: no remote copies, remote signals or barrier semaphores. Data moves between devices by JAX's collectives and lax.ppermute only.
A program may use at most 64 MiB of HBM per device.

v0:
```python
import jax
import jax.numpy as jnp
from jax import lax
from jax.sharding import PartitionSpec as P


def with_halo(value, sides, width):
    for axis, dim in sides:
        size, length = (lax.axis_size(axis), value.shape[dim])
        up = [(i, (i + 1) % size) for i in range(size - 1)]
        down = [(j, i) for i, j in up]
        last = lax.slice_in_dim(value, length - width, length, axis=dim)
        initial = lax.slice_in_dim(value, 0, width, axis=dim)
        before = lax.ppermute(last, axis, up)
        after = lax.ppermute(initial, axis, down)
        value = jnp.concatenate([before, value, after], axis=dim)
    return value


def band_table(width):
    source = lax.broadcasted_iota(jnp.int32, (width + 2, 3, width), 0)
    offsets = lax.broadcasted_iota(jnp.int32, (width + 2, 3, width), 1)
    target = lax.broadcasted_iota(jnp.int32, (width + 2, 3, width), 2)
    return jnp.where(source == target + offsets, 1.0, 0.0).astype(jnp.bfloat16)


def convolve(field, kernel, offset):
    padded = with_halo(field, (("gx", 1), ("gy", 2), ("gz", 3)), 1)
    depth = field.shape[1]
    height = field.shape[2]
    width = field.shape[3]
    shifted = jnp.einsum(
        "cxyw,wdz->dcxyz", padded, band_table(width), preferred_element_type=jnp.float32
    ).astype(jnp.bfloat16)
    linear = jnp.zeros((kernel.shape[0], depth, height, width), jnp.float32)
    for step_x in range(3):
        for step_y in range(3):
            slab = shifted[:, :, step_x : step_x + depth, step_y : step_y + height, :]
            taps = kernel[:, :, step_x, step_y, :]
            linear = linear + jnp.einsum(
                "oid,dixyz->oxyz", taps, slab, preferred_element_type=jnp.float32
            )
    summed = linear + offset.astype(jnp.float32)[:, None, None, None]
    return jnp.where(summed > 0, summed, 0.2 * summed).astype(jnp.bfloat16)


def section_pass(field, kernels, offsets):
    return convolve(convolve(field, kernels[0], offsets[0]), kernels[1], offsets[1])


def shards(features, weights, biases):
    section = lax.axis_index("segment")
    micro_count = features.shape[0]
    all_kernels, all_offsets = (
        lax.all_gather(weights, "segment", axis=0, tiled=True),
        lax.all_gather(biases, "segment", axis=0, tiled=True),
    )
    half_count = micro_count // 2
    my_batches = lax.dynamic_slice_in_dim(features, section * half_count, half_count, 0)
    hidden = section_pass(my_batches[0], all_kernels[0], all_offsets[0])
    first_list = [hidden]
    hidden = section_pass(hidden, all_kernels[1], all_offsets[1])
    second_list = [hidden]
    stacked = jnp.stack([jnp.stack(first_list), jnp.stack(second_list)])
    return lax.all_to_all(stacked, "segment", split_axis=0, concat_axis=1, tiled=True)


def solution(mesh):
    placed = (
        P(None, None, "gx", "gy", "gz"),
        P("segment", None, None, None, None, None, None),
        P("segment", None, None),
    )
    return jax.shard_map(
        shards,
        mesh=mesh,
        in_specs=placed,
        out_specs=P("segment", None, None, "gx", "gy", "gz"),
        check_vma=False,
    )
```

profile of v0, /device:TPU:0, one launch (start us, length us, event | category | flops | bytes accessed | tf_op | source)
XLA Modules:
  0.0 191.6 jit_solution(2719549731387878683)
XLA Ops:
  1.3 4.9 %collective-permute-start = (bf16[16,1,32,128]{3,2,1,0:T(8,128)(2,1)S(1)}, bf16[16,1,32,128]{3,2,1,0:T(8,128)(2,1)S(1)}, u32[]{:S(2)}, u32[]{:S(2)}) collective-permute-start(bf16[16,1,32,128]{3,2,1,0:T(8,128)(2,1)S(1)} %get-tuple-element.63), channel_id=1, source_target_pairs={{0,8},{1,9},{2,10},{3,11},{4,12},{5,13},{6,14},{7,15},{16,24},{17,... | collective-permute-start | bytes 393224 | tf_op jit(solution)/shard_map/ppermute | solution.py:14
  7.5 2.1 %all_gather.6 = bf16[2,2,16,16,3,3,3]{3,2,6,5,4,1,0:T(8,128)(2,1)S(1)} all-gather(bf16[1,2,16,16,3,3,3]{3,2,6,5,4,1,0:T(8,128)(2,1)S(1)} %copy-done.2), channel_id=1, replica_groups=mesh['segment'=2,'gx'=2,'gy'=4,'gz'=2] {'segment'}, dimensions={0}, use_global_device_ids=true | all-gather | bytes 82944 | tf_op jit(solution)/shard_map/all_gather | solution.py:55
  9.6 3.4 %collective-permute-done.1 = bf16[16,1,32,128]{3,2,1,0:T(8,128)(2,1)S(1)} collective-permute-done((bf16[16,1,32,128]{3,2,1,0:T(8,128)(2,1)S(1)}, bf16[16,1,32,128]{3,2,1,0:T(8,128)(2,1)S(1)}, u32[]{:S(2)}, u32[]{:S(2)}) %collective-permute-start.1) | collective-permute-done | bytes 131104 | tf_op jit(solution)/shard_map/ppermute | solution.py:15
  13.1 3.5 %collective-permute-start.2 = (bf16[16,6,1,128]{3,2,1,0:T(2,128)(2,1)S(1)}, bf16[16,6,1,128]{3,2,1,0:T(2,128)(2,1)S(1)}, u32[]{:S(2)}, u32[]{:S(2)}) collective-permute-start(bf16[16,6,1,128]{3,2,1,0:T(2,128)(2,1)S(1)} %get-tuple-element.55), channel_id=1, source_target_pairs={{0,2},{2,4},{4,6},{1,3},{3,5},{5,7},{8,10},{10,12},{12,14},{9,11},... | collective-permute-start | bytes 73736 | tf_op jit(solution)/shard_map/ppermute | solution.py:14
  18.0 1.8 all_gather.7
  19.8 2.8 %collective-permute-done.3 = bf16[16,6,1,128]{3,2,1,0:T(2,128)(2,1)S(1)} collective-permute-done((bf16[16,6,1,128]{3,2,1,0:T(2,128)(2,1)S(1)}, bf16[16,6,1,128]{3,2,1,0:T(2,128)(2,1)S(1)}, u32[]{:S(2)}, u32[]{:S(2)}) %collective-permute-start.3) | collective-permute-done | bytes 24608 | tf_op jit(solution)/shard_map/ppermute | solution.py:15
  26.2 4.5 %collective-permute-start.4 = (bf16[16,6,34,1]{2,0,3,1:T(8,128)(2,1)S(1)}, bf16[16,6,34,1]{2,0,3,1:T(8,128)(2,1)S(1)}, u32[]{:S(2)}, u32[]{:S(2)}) collective-permute-start(bf16[16,6,34,1]{2,0,3,1:T(8,128)(2,1)S(1)} %copy.44), channel_id=1, source_target_pairs={{0,1},{2,3},{4,5},{6,7},{8,9},{10,11},{12,13},{14,15},{16,17},{18,... | collective-permute-start | bytes 19592 | tf_op jit(solution)/shard_map/ppermute | solution.py:14
  33.8 2.9 %convert_bitcast_fusion.3 = bf16[3,16,6,34,128]{4,3,2,1,0:T(8,128)(2,1)S(1)} fusion(bf16[16,6,34,1]{3,2,1,0:T(8,128)(2,1)S(1)} %copy.47, bf16[16,6,1,128]{3,2,1,0:T(2,128)(2,1)S(1)} %collective-permute-done.3, bf16[16,1,32,128]{3,2,1,0:T(8,128)(2,1)S(1)} %collective-permute-done.1, bf16[16,4,32,128]{3,2,1,0:T(8,128)(2,1)S(1)} %dynamic-slice_bitcast_fusion, ...), kind=kOutput, calls=%fused_computation.7 | convolution fusion | flops 333271296 | bytes 3355392 | tf_op jit(solution)/shard_map/cxyw,wdz->dcxyz/dot_general | solution.py:32
  36.7 3.7 %fusion.370 = (bf16[3,16,4,32,128]{4,3,2,1,0:T(8,128)(2,1)S(1)}, bf16[3,16,4,32,128]{4,3,2,1,0:T(8,128)(2,1)S(1)}, bf16[3,16,4,32,128]{4,3,2,1,0:T(8,128)(2,1)S(...) fusion(bf16[3,16,6,34,128]{4,3,2,1,0:T(8,128)(2,1)S(1)} %conver, ...), kind=kLoop, calls=%fused_computation.272 | loop fusion | bytes 28311552 | tf_op jit(solution)/shard_map/slice | solution.py:38
  54.1 4.4 %collective-permute-done.7 = bf16[16,1,32,128]{3,0,2,1:T(8,128)(2,1)S(1)} collective-permute-done((bf16[16,1,32,128]{3,0,2,1:T(8,128)(2,1)S(1)}, bf16[16,1,32,128]{3,0,2,1:T(8,128)(2,1)S(1)}, u32[]{:S(2)}, u32[]{:S(2)}) %collective-permute-start.7) | collective-permute-done | bytes 131104 | tf_op jit(solution)/shard_map/ppermute | solution.py:15
  58.4 3.5 %collective-permute-start.8 = (bf16[16,6,1,128]{3,0,2,1:T(8,128)(2,1)S(1)}, bf16[16,6,1,128]{3,0,2,1:T(8,128)(2,1)S(1)}, u32[]{:S(2)}, u32[]{:S(2)}) collective-permute-start(bf16[16,6,1,128]{3,0,2,1:T(8,128)(2,1)S(1)} %get-tuple-element.53), channel_id=1, source_target_pairs={{0,2},{2,4},{4,6},{1,3},{3,5},{5,7},{8,10},{10,12},{12,14},{9,11},... | collective-permute-start | bytes 73736 | tf_op jit(solution)/shard_map/ppermute | solution.py:14
  61.9 1.5 collective-permute-start.9
  63.5 4.2 %collective-permute-done.9 = bf16[16,6,1,128]{3,0,2,1:T(8,128)(2,1)S(1)} collective-permute-done((bf16[16,6,1,128]{3,0,2,1:T(8,128)(2,1)S(1)}, bf16[16,6,1,128]{3,0,2,1:T(8,128)(2,1)S(1)}, u32[]{:S(2)}, u32[]{:S(2)}) %collective-permute-start.9) | collective-permute-done | bytes 24608 | tf_op jit(solution)/shard_map/ppermute | solution.py:15
  69.1 4.2 %collective-permute-start.10 = (bf16[16,6,34,1]{2,0,3,1:T(8,128)(2,1)S(1)}, bf16[16,6,34,1]{2,0,3,1:T(8,128)(2,1)S(1)}, u32[]{:S(2)}, u32[]{:S(2)}) collective-permute-start(bf16[16,6,34,1]{2,0,3,1:T(8,128)(2,1)S(1)} %copy.57), channel_id=1, source_target_pairs={{0,1},{2,3},{4,5},{6,7},{8,9},{10,11},{12,13},{14,15},{16,17},{18,... | collective-permute-start | bytes 19592 | tf_op jit(solution)/shard_map/ppermute | solution.py:14
  76.3 3.6 %collective-permute-done.11 = bf16[16,6,34,1]{2,0,3,1:T(8,128)(2,1)S(1)} collective-permute-done((bf16[16,6,34,1]{2,0,3,1:T(8,128)(2,1)S(1)}, bf16[16,6,34,1]{2,0,3,1:T(8,128)(2,1)S(1)}, u32[]{:S(2)}, u32[]{:S(2)}) %collective-permute-start.11) | collective-permute-done | bytes 6560 | tf_op jit(solution)/shard_map/ppermute | solution.py:15
  80.7 1.9 pad_maximum_fusion
  84.0 4.1 %fusion.369 = (bf16[3,16,4,32,128]{4,3,2,1,0:T(8,128)(2,1)S(1)}, bf16[3,16,4,32,128]{4,3,2,1,0:T(8,128)(2,1)S(1)}, bf16[3,16,4,32,128]{4,3,2,1,0:T(8,128)(2,1)S(...) fusion(bf16[3,16,6,34,128]{4,3,2,1,0:T(8,128)(2,1)S(1)} %conver, ...), kind=kLoop, calls=%fused_computation.271 | loop fusion | bytes 28311552 | tf_op jit(solution)/shard_map/slice | solution.py:38
  101.7 4.4 %collective-permute-done.13 = bf16[16,1,32,128]{3,0,2,1:T(8,128)(2,1)S(1)} collective-permute-done((bf16[16,1,32,128]{3,0,2,1:T(8,128)(2,1)S(1)}, bf16[16,1,32,128]{3,0,2,1:T(8,128)(2,1)S(1)}, u32[]{:S(2)}, u32[]{:S(2)}) %collective-permute-start.13) | collective-permute-done | bytes 131104 | tf_op jit(solution)/shard_map/ppermute | solution.py:15
  106.1 3.5 %collective-permute-start.14 = (bf16[16,6,1,128]{3,0,2,1:T(8,128)(2,1)S(1)}, bf16[16,6,1,128]{3,0,2,1:T(8,128)(2,1)S(1)}, u32[]{:S(2)}, u32[]{:S(2)}) collective-permute-start(bf16[16,6,1,128]{3,0,2,1:T(8,128)(2,1)S(1)} %get-tuple-element.51), channel_id=1, source_target_pairs={{0,2},{2,4},{4,6},{1,3},{3,5},{5,7},{8,10},{10,12},{12,14},{9,11},... | collective-permute-start | bytes 73736 | tf_op jit(solution)/shard_map/ppermute | solution.py:14
  111.1 4.2 %collective-permute-done.15 = bf16[16,6,1,128]{3,0,2,1:T(8,128)(2,1)S(1)} collective-permute-done((bf16[16,6,1,128]{3,0,2,1:T(8,128)(2,1)S(1)}, bf16[16,6,1,128]{3,0,2,1:T(8,128)(2,1)S(1)}, u32[]{:S(2)}, u32[]{:S(2)}) %collective-permute-start.15) | collective-permute-done | bytes 24608 | tf_op jit(solution)/shard_map/ppermute | solution.py:15
  116.7 1.6 collective-permute-start.16
  121.5 3.4 %collective-permute-done.17 = bf16[16,6,34,1]{2,0,3,1:T(8,128)(2,1)S(1)} collective-permute-done((bf16[16,6,34,1]{2,0,3,1:T(8,128)(2,1)S(1)}, bf16[16,6,34,1]{2,0,3,1:T(8,128)(2,1)S(1)}, u32[]{:S(2)}, u32[]{:S(2)}) %collective-permute-start.17) | collective-permute-done | bytes 6560 | tf_op jit(solution)/shard_map/ppermute | solution.py:15
  125.8 1.9 pad_maximum_fusion.1
  129.0 3.7 %fusion.368 = (bf16[3,16,4,32,128]{4,3,2,1,0:T(8,128)(2,1)S(1)}, bf16[3,16,4,32,128]{4,3,2,1,0:T(8,128)(2,1)S(1)}, bf16[3,16,4,32,128]{4,3,2,1,0:T(8,128)(2,1)S(...) fusion(bf16[3,16,6,34,128]{4,3,2,1,0:T(8,128)(2,1)S(1)} %conver, ...), kind=kLoop, calls=%fused_computation.270 | loop fusion | bytes 28311552 | tf_op jit(solution)/shard_map/slice | solution.py:38
  146.3 4.4 %collective-permute-done.19 = bf16[16,1,32,128]{3,0,2,1:T(8,128)(2,1)S(1)} collective-permute-done((bf16[16,1,32,128]{3,0,2,1:T(8,128)(2,1)S(1)}, bf16[16,1,32,128]{3,0,2,1:T(8,128)(2,1)S(1)}, u32[]{:S(2)}, u32[]{:S(2)}) %collective-permute-start.19) | collective-permute-done | bytes 131104 | tf_op jit(solution)/shard_map/ppermute | solution.py:15
  150.7 1.9 %collective-permute-start.20 = (bf16[16,6,1,128]{3,0,2,1:T(8,128)(2,1)S(1)}, bf16[16,6,1,128]{3,0,2,1:T(8,128)(2,1)S(1)}, u32[]{:S(2)}, u32[]{:S(2)}) collective-permute-start(bf16[16,6,1,128]{3,0,2,1:T(8,128)(2,1)S(1)} %get-tuple-element.49), channel_id=1, source_target_pairs={{0,2},{2,4},{4,6},{1,3},{3,5},{5,7},{8,10},{10,12},{12,14},{9,11},... | collective-permute-start | bytes 73736 | tf_op jit(solution)/shard_map/ppermute | solution.py:14
  154.1 4.2 %collective-permute-done.21 = bf16[16,6,1,128]{3,0,2,1:T(8,128)(2,1)S(1)} collective-permute-done((bf16[16,6,1,128]{3,0,2,1:T(8,128)(2,1)S(1)}, bf16[16,6,1,128]{3,0,2,1:T(8,128)(2,1)S(1)}, u32[]{:S(2)}, u32[]{:S(2)}) %collective-permute-start.21) | collective-permute-done | bytes 24608 | tf_op jit(solution)/shard_map/ppermute | solution.py:15
  159.8 1.6 collective-permute-start.22
  164.6 3.4 %collective-permute-done.23 = bf16[16,6,34,1]{2,0,3,1:T(8,128)(2,1)S(1)} collective-permute-done((bf16[16,6,34,1]{2,0,3,1:T(8,128)(2,1)S(1)}, bf16[16,6,34,1]{2,0,3,1:T(8,128)(2,1)S(1)}, u32[]{:S(2)}, u32[]{:S(2)}) %collective-permute-start.23) | collective-permute-done | bytes 6560 | tf_op jit(solution)/shard_map/ppermute | solution.py:15
  168.8 1.9 pad_maximum_fusion.2
  172.1 3.7 %fusion.367 = (bf16[3,16,4,32,128]{4,3,2,1,0:T(8,128)(2,1)S(1)}, bf16[3,16,4,32,128]{4,3,2,1,0:T(8,128)(2,1)S(1)}, bf16[3,16,4,32,128]{4,3,2,1,0:T(8,128)(2,1)S(...) fusion(bf16[3,16,6,34,128]{4,3,2,1,0:T(8,128)(2,1)S(1)} %conver, ...), kind=kLoop, calls=%fused_computation.269 | loop fusion | bytes 28311552 | tf_op jit(solution)/shard_map/slice | solution.py:38
  185.4 4.7 %all_to_all.12 = bf16[2,1,16,4,32,128]{5,2,4,3,1,0:T(8,128)(2,1)S(1)} all-to-all(bf16[2,1,16,4,32,128]{5,2,4,3,1,0:T(8,128)(2,1)S(1)} %pad_maximum_fusion.3), channel_id=1, replica_groups=mesh['segment'=2,'gx'=2,'gy'=4,'gz'=2] {'segment'}, dimensions={0} | all-to-all | bytes 2097152 | tf_op jit(solution)/shard_map/all_to_all | solution.py:65
  (111 shorter events, 85.5 us)
Async XLA Ops:
  0.0 1.2 copy-start
  0.0 7.5 %copy-start.2 = (bf16[1,2,16,16,3,3,3]{3,2,6,5,4,1,0:T(8,128)(2,1)S(1)}, bf16[1,2,16,16,3,3,3]{3,2,6,5,4,1,0:T(8,128)(2,1)}, u32[]{:S(2)}) copy-start(bf16[1,2,16,16,3,3,3]{3,2,6,5,4,1,0:T(8,128)(2,1)} %param.4) | copy-start | bytes 82948
  1.3 16.7 %copy-start.3 = (bf16[1,2,16]{2,1,0:T(2,128)(2,1)S(1)}, bf16[1,2,16]{2,1,0:T(2,128)(2,1)}, u32[]{:S(2)}) copy-start(bf16[1,2,16]{2,1,0:T(2,128)(2,1)} %param.5) | copy-start | bytes 196
  1.3 8.3 %collective-permute-start = (bf16[16,1,32,128]{3,2,1,0:T(8,128)(2,1)S(1)}, bf16[16,1,32,128]{3,2,1,0:T(8,128)(2,1)S(1)}, u32[]{:S(2)}, u32[]{:S(2)}) collective-permute-start(bf16[16,1,32,128]{3,2,1,0:T(8,128)(2,1)S(1)} %get-tuple-element.63), channel_id=1, source_target_pairs={{0,8},{1,9},{2,10},{3,11},{4,12},{5,13},{6,14},{7,15},{16,24},{17,... | collective-permute-start | bytes 393224 | tf_op jit(solution)/shard_map/ppermute | solution.py:14
  6.2 6.9 %collective-permute-start.1 = (bf16[16,1,32,128]{3,2,1,0:T(8,128)(2,1)S(1)}, bf16[16,1,32,128]{3,2,1,0:T(8,128)(2,1)S(1)}, u32[]{:S(2)}, u32[]{:S(2)}) collective-permute-start(bf16[16,1,32,128]{3,2,1,0:T(8,128)(2,1)S(1)} %get-tuple-element.64), channel_id=1, source_target_pairs={{8,0},{9,1},{10,2},{11,3},{12,4},{13,5},{14,6},{15,7},{24,16},{25,... | collective-permute-start | bytes 393224 | tf_op jit(solution)/shard_map/ppermute | solution.py:15
  13.1 6.7 %collective-permute-start.2 = (bf16[16,6,1,128]{3,2,1,0:T(2,128)(2,1)S(1)}, bf16[16,6,1,128]{3,2,1,0:T(2,128)(2,1)S(1)}, u32[]{:S(2)}, u32[]{:S(2)}) collective-permute-start(bf16[16,6,1,128]{3,2,1,0:T(2,128)(2,1)S(1)} %get-tuple-element.55), channel_id=1, source_target_pairs={{0,2},{2,4},{4,6},{1,3},{3,5},{5,7},{8,10},{10,12},{12,14},{9,11},... | collective-permute-start | bytes 73736 | tf_op jit(solution)/shard_map/ppermute | solution.py:14
  16.6 6.0 %collective-permute-start.3 = (bf16[16,6,1,128]{3,2,1,0:T(2,128)(2,1)S(1)}, bf16[16,6,1,128]{3,2,1,0:T(2,128)(2,1)S(1)}, u32[]{:S(2)}, u32[]{:S(2)}) collective-permute-start(bf16[16,6,1,128]{3,2,1,0:T(2,128)(2,1)S(1)} %get-tuple-element.56), channel_id=1, source_target_pairs={{2,0},{4,2},{6,4},{3,1},{5,3},{7,5},{10,8},{12,10},{14,12},{11,9},... | collective-permute-start | bytes 73736 | tf_op jit(solution)/shard_map/ppermute | solution.py:15
  24.9 8.1 %collective-permute-start.5 = (bf16[16,6,34,1]{2,0,3,1:T(8,128)(2,1)S(1)}, bf16[16,6,34,1]{2,0,3,1:T(8,128)(2,1)S(1)}, u32[]{:S(2)}, u32[]{:S(2)}) collective-permute-start(bf16[16,6,34,1]{2,0,3,1:T(8,128)(2,1)S(1)} %copy.45), channel_id=1, source_target_pairs={{1,0},{3,2},{5,4},{7,6},{9,8},{11,10},{13,12},{15,14},{17,16},{19,... | collective-permute-start | bytes 19592 | tf_op jit(solution)/shard_map/ppermute | solution.py:15
  26.2 6.1 %collective-permute-start.4 = (bf16[16,6,34,1]{2,0,3,1:T(8,128)(2,1)S(1)}, bf16[16,6,34,1]{2,0,3,1:T(8,128)(2,1)S(1)}, u32[]{:S(2)}, u32[]{:S(2)}) collective-permute-start(bf16[16,6,34,1]{2,0,3,1:T(8,128)(2,1)S(1)} %copy.44), channel_id=1, source_target_pairs={{0,1},{2,3},{4,5},{6,7},{8,9},{10,11},{12,13},{14,15},{16,17},{18,... | collective-permute-start | bytes 19592 | tf_op jit(solution)/shard_map/ppermute | solution.py:14
  50.1 4.0 %collective-permute-start.6 = (bf16[16,1,32,128]{3,0,2,1:T(8,128)(2,1)S(1)}, bf16[16,1,32,128]{3,0,2,1:T(8,128)(2,1)S(1)}, u32[]{:S(2)}, u32[]{:S(2)}) collective-permute-start(bf16[16,1,32,128]{3,0,2,1:T(8,128)(2,1)S(1)} %get-tuple-element.61), channel_id=1, source_target_pairs={{0,8},{1,9},{2,10},{3,11},{4,12},{5,13},{6,14},{7,15},{16,24},{17,... | collective-permute-start | bytes 393224 | tf_op jit(solution)/shard_map/ppermute | solution.py:14
  51.6 6.9 %collective-permute-start.7 = (bf16[16,1,32,128]{3,0,2,1:T(8,128)(2,1)S(1)}, bf16[16,1,32,128]{3,0,2,1:T(8,128)(2,1)S(1)}, u32[]{:S(2)}, u32[]{:S(2)}) collective-permute-start(bf16[16,1,32,128]{3,0,2,1:T(8,128)(2,1)S(1)} %get-tuple-element.62), channel_id=1, source_target_pairs={{8,0},{9,1},{10,2},{11,3},{12,4},{13,5},{14,6},{15,7},{24,16},{25,... | collective-permute-start | bytes 393224 | tf_op jit(solution)/shard_map/ppermute | solution.py:15
  58.4 5.0 %collective-permute-start.8 = (bf16[16,6,1,128]{3,0,2,1:T(8,128)(2,1)S(1)}, bf16[16,6,1,128]{3,0,2,1:T(8,128)(2,1)S(1)}, u32[]{:S(2)}, u32[]{:S(2)}) collective-permute-start(bf16[16,6,1,128]{3,0,2,1:T(8,128)(2,1)S(1)} %get-tuple-element.53), channel_id=1, source_target_pairs={{0,2},{2,4},{4,6},{1,3},{3,5},{5,7},{8,10},{10,12},{12,14},{9,11},... | collective-permute-start | bytes 73736 | tf_op jit(solution)/shard_map/ppermute | solution.py:14
  61.9 5.7 %collective-permute-start.9 = (bf16[16,6,1,128]{3,0,2,1:T(8,128)(2,1)S(1)}, bf16[16,6,1,128]{3,0,2,1:T(8,128)(2,1)S(1)}, u32[]{:S(2)}, u32[]{:S(2)}) collective-permute-start(bf16[16,6,1,128]{3,0,2,1:T(8,128)(2,1)S(1)} %get-tuple-element.54), channel_id=1, source_target_pairs={{2,0},{4,2},{6,4},{3,1},{5,3},{7,5},{10,8},{12,10},{14,12},{11,9},... | collective-permute-start | bytes 73736 | tf_op jit(solution)/shard_map/ppermute | solution.py:15
  69.1 6.4 %collective-permute-start.10 = (bf16[16,6,34,1]{2,0,3,1:T(8,128)(2,1)S(1)}, bf16[16,6,34,1]{2,0,3,1:T(8,128)(2,1)S(1)}, u32[]{:S(2)}, u32[]{:S(2)}) collective-permute-start(bf16[16,6,34,1]{2,0,3,1:T(8,128)(2,1)S(1)} %copy.57), channel_id=1, source_target_pairs={{0,1},{2,3},{4,5},{6,7},{8,9},{10,11},{12,13},{14,15},{16,17},{18,... | collective-permute-start | bytes 19592 | tf_op jit(solution)/shard_map/ppermute | solution.py:14
  74.2 5.7 %collective-permute-start.11 = (bf16[16,6,34,1]{2,0,3,1:T(8,128)(2,1)S(1)}, bf16[16,6,34,1]{2,0,3,1:T(8,128)(2,1)S(1)}, u32[]{:S(2)}, u32[]{:S(2)}) collective-permute-start(bf16[16,6,34,1]{2,0,3,1:T(8,128)(2,1)S(1)} %copy.58), channel_id=1, source_target_pairs={{1,0},{3,2},{5,4},{7,6},{9,8},{11,10},{13,12},{15,14},{17,16},{19,... | collective-permute-start | bytes 19592 | tf_op jit(solution)/shard_map/ppermute | solution.py:15
  97.7 4.0 %collective-permute-start.12 = (bf16[16,1,32,128]{3,0,2,1:T(8,128)(2,1)S(1)}, bf16[16,1,32,128]{3,0,2,1:T(8,128)(2,1)S(1)}, u32[]{:S(2)}, u32[]{:S(2)}) collective-permute-start(bf16[16,1,32,128]{3,0,2,1:T(8,128)(2,1)S(1)} %get-tuple-element.59), channel_id=1, source_target_pairs={{0,8},{1,9},{2,10},{3,11},{4,12},{5,13},{6,14},{7,15},{16,24},{17,... | collective-permute-start | bytes 393224 | tf_op jit(solution)/shard_map/ppermute | solution.py:14
  99.2 6.9 %collective-permute-start.13 = (bf16[16,1,32,128]{3,0,2,1:T(8,128)(2,1)S(1)}, bf16[16,1,32,128]{3,0,2,1:T(8,128)(2,1)S(1)}, u32[]{:S(2)}, u32[]{:S(2)}) collective-permute-start(bf16[16,1,32,128]{3,0,2,1:T(8,128)(2,1)S(1)} %get-tuple-element.60), channel_id=1, source_target_pairs={{8,0},{9,1},{10,2},{11,3},{12,4},{13,5},{14,6},{15,7},{24,16},{25,... | collective-permute-start | bytes 393224 | tf_op jit(solution)/shard_map/ppermute | solution.py:15
  106.1 5.0 %collective-permute-start.14 = (bf16[16,6,1,128]{3,0,2,1:T(8,128)(2,1)S(1)}, bf16[16,6,1,128]{3,0,2,1:T(8,128)(2,1)S(1)}, u32[]{:S(2)}, u32[]{:S(2)}) collective-permute-start(bf16[16,6,1,128]{3,0,2,1:T(8,128)(2,1)S(1)} %get-tuple-element.51), channel_id=1, source_target_pairs={{0,2},{2,4},{4,6},{1,3},{3,5},{5,7},{8,10},{10,12},{12,14},{9,11},... | collective-permute-start | bytes 73736 | tf_op jit(solution)/shard_map/ppermute | solution.py:14
  109.6 5.7 %collective-permute-start.15 = (bf16[16,6,1,128]{3,0,2,1:T(8,128)(2,1)S(1)}, bf16[16,6,1,128]{3,0,2,1:T(8,128)(2,1)S(1)}, u32[]{:S(2)}, u32[]{:S(2)}) collective-permute-start(bf16[16,6,1,128]{3,0,2,1:T(8,128)(2,1)S(1)} %get-tuple-element.52), channel_id=1, source_target_pairs={{2,0},{4,2},{6,4},{3,1},{5,3},{7,5},{10,8},{12,10},{14,12},{11,9},... | collective-permute-start | bytes 73736 | tf_op jit(solution)/shard_map/ppermute | solution.py:15
  116.7 4.0 %collective-permute-start.16 = (bf16[16,6,34,1]{2,0,3,1:T(8,128)(2,1)S(1)}, bf16[16,6,34,1]{2,0,3,1:T(8,128)(2,1)S(1)}, u32[]{:S(2)}, u32[]{:S(2)}) collective-permute-start(bf16[16,6,34,1]{2,0,3,1:T(8,128)(2,1)S(1)} %copy.71), channel_id=1, source_target_pairs={{0,1},{2,3},{4,5},{6,7},{8,9},{10,11},{12,13},{14,15},{16,17},{18,... | collective-permute-start | bytes 19592 | tf_op jit(solution)/shard_map/ppermute | solution.py:14
  119.2 5.7 %collective-permute-start.17 = (bf16[16,6,34,1]{2,0,3,1:T(8,128)(2,1)S(1)}, bf16[16,6,34,1]{2,0,3,1:T(8,128)(2,1)S(1)}, u32[]{:S(2)}, u32[]{:S(2)}) collective-permute-start(bf16[16,6,34,1]{2,0,3,1:T(8,128)(2,1)S(1)} %copy.72), channel_id=1, source_target_pairs={{1,0},{3,2},{5,4},{7,6},{9,8},{11,10},{13,12},{15,14},{17,16},{19,... | collective-permute-start | bytes 19592 | tf_op jit(solution)/shard_map/ppermute | solution.py:15
  142.3 4.0 %collective-permute-start.18 = (bf16[16,1,32,128]{3,0,2,1:T(8,128)(2,1)S(1)}, bf16[16,1,32,128]{3,0,2,1:T(8,128)(2,1)S(1)}, u32[]{:S(2)}, u32[]{:S(2)}) collective-permute-start(bf16[16,1,32,128]{3,0,2,1:T(8,128)(2,1)S(1)} %get-tuple-element.57), channel_id=1, source_target_pairs={{0,8},{1,9},{2,10},{3,11},{4,12},{5,13},{6,14},{7,15},{16,24},{17,... | collective-permute-start | bytes 393224 | tf_op jit(solution)/shard_map/ppermute | solution.py:14
  143.8 6.9 %collective-permute-start.19 = (bf16[16,1,32,128]{3,0,2,1:T(8,128)(2,1)S(1)}, bf16[16,1,32,128]{3,0,2,1:T(8,128)(2,1)S(1)}, u32[]{:S(2)}, u32[]{:S(2)}) collective-permute-start(bf16[16,1,32,128]{3,0,2,1:T(8,128)(2,1)S(1)} %get-tuple-element.58), channel_id=1, source_target_pairs={{8,0},{9,1},{10,2},{11,3},{12,4},{13,5},{14,6},{15,7},{24,16},{25,... | collective-permute-start | bytes 393224 | tf_op jit(solution)/shard_map/ppermute | solution.py:15
  150.7 3.4 %collective-permute-start.20 = (bf16[16,6,1,128]{3,0,2,1:T(8,128)(2,1)S(1)}, bf16[16,6,1,128]{3,0,2,1:T(8,128)(2,1)S(1)}, u32[]{:S(2)}, u32[]{:S(2)}) collective-permute-start(bf16[16,6,1,128]{3,0,2,1:T(8,128)(2,1)S(1)} %get-tuple-element.49), channel_id=1, source_target_pairs={{0,2},{2,4},{4,6},{1,3},{3,5},{5,7},{8,10},{10,12},{12,14},{9,11},... | collective-permute-start | bytes 73736 | tf_op jit(solution)/shard_map/ppermute | solution.py:14
  152.6 5.7 %collective-permute-start.21 = (bf16[16,6,1,128]{3,0,2,1:T(8,128)(2,1)S(1)}, bf16[16,6,1,128]{3,0,2,1:T(8,128)(2,1)S(1)}, u32[]{:S(2)}, u32[]{:S(2)}) collective-permute-start(bf16[16,6,1,128]{3,0,2,1:T(8,128)(2,1)S(1)} %get-tuple-element.50), channel_id=1, source_target_pairs={{2,0},{4,2},{6,4},{3,1},{5,3},{7,5},{10,8},{12,10},{14,12},{11,9},... | collective-permute-start | bytes 73736 | tf_op jit(solution)/shard_map/ppermute | solution.py:15
  159.8 4.0 %collective-permute-start.22 = (bf16[16,6,34,1]{2,0,3,1:T(8,128)(2,1)S(1)}, bf16[16,6,34,1]{2,0,3,1:T(8,128)(2,1)S(1)}, u32[]{:S(2)}, u32[]{:S(2)}) collective-permute-start(bf16[16,6,34,1]{2,0,3,1:T(8,128)(2,1)S(1)} %copy.85), channel_id=1, source_target_pairs={{0,1},{2,3},{4,5},{6,7},{8,9},{10,11},{12,13},{14,15},{16,17},{18,... | collective-permute-start | bytes 19592 | tf_op jit(solution)/shard_map/ppermute | solution.py:14
  162.2 5.7 %collective-permute-start.23 = (bf16[16,6,34,1]{2,0,3,1:T(8,128)(2,1)S(1)}, bf16[16,6,34,1]{2,0,3,1:T(8,128)(2,1)S(1)}, u32[]{:S(2)}, u32[]{:S(2)}) collective-permute-start(bf16[16,6,34,1]{2,0,3,1:T(8,128)(2,1)S(1)} %copy.86), channel_id=1, source_target_pairs={{1,0},{3,2},{5,4},{7,6},{9,8},{11,10},{13,12},{15,14},{17,16},{19,... | collective-permute-start | bytes 19592 | tf_op jit(solution)/shard_map/ppermute | solution.py:15
  185.4 6.0 %copy-start.1 = (bf16[2,16,4,32,128]{4,3,2,1,0:T(8,128)(2,1)S(1)}, bf16[2,16,4,32,128]{4,3,2,1,0:T(8,128)(2,1)}, u32[]{:S(2)}) copy-start(bf16[2,16,4,32,128]{4,3,2,1,0:T(8,128)(2,1)} %param.3) | copy-start | bytes 3145732
where the time goes:
time: 195 us; the launch traced here: 192 us
  starting transfers between devices  49.8 us (26%)
  waiting for transfers between devices  47.8 us (25%)
  matrix products  45.5 us (23%)
  local copies, waits for them, and re-layouts  32.2 us (17%)
  blocking collectives  8.64 us (4%)
  other arithmetic  6.92 us (4%)
    ppermute x12, waiting for transfers between devices, with_halo(): after = lax.ppermute(initial, axis, down)  42.3 us
    dot_general x36, matrix products, convolve(): jnp.einsum('oid,dixyz->oxyz', taps, slab, preferred_element_type=jnp.floa...  38.4 us
    ppermute x12, starting transfers between devices, with_halo(): before = lax.ppermute(last, axis, up)  33.7 us
    ppermute x12, starting transfers between devices, with_halo(): after = lax.ppermute(initial, axis, down)  16.1 us
    slice x4, local copies, waits for them, and re-layouts, convolve(): slab = shifted[:, :, step_x:step_x + depth, step_y:step_y + height, :]  15 us
    dot_general x4, matrix products, convolve(): jnp.einsum('cxyw,wdz->dcxyz', padded, band_table(width), preferred_elemen...  7.04 us
    concatenate x7, other arithmetic, with_halo(): value = jnp.concatenate([before, value, after], axis=dim)  6.71 us
    ppermute x12, waiting for transfers between devices, with_halo(): before = lax.ppermute(last, axis, up)  5.5 us
  transfers between devices with their start and end apart: 24, of which 17 were waited for; matrix products, arithmetic and copies ran while one was open for 3% of the time, Pallas kernels for 0%

commit v1 on v0

--- a/solution.py
+++ b/solution.py
@@ -62,7 +62,12 @@
     hidden = section_pass(hidden, all_kernels[1], all_offsets[1])
     second_list = [hidden]
     stacked = jnp.stack([jnp.stack(first_list), jnp.stack(second_list)])
-    return lax.all_to_all(stacked, "segment", split_axis=0, concat_axis=1, tiled=True)
+    return jnp.concatenate(
+        lax.all_to_all(
+            jnp.stack(jnp.split(stacked, lax.axis_size("segment"), axis=0)), "segment", 0, 0
+        ),
+        axis=1,
+    )
 
 
 def solution(mesh):

time: 195 us -> 195 us (level)
  no operation moved by 1% of the time
where the time goes in v1:
time: 195 us; the launch traced here: 192 us
  starting transfers between devices  49.8 us (26%)
  waiting for transfers between devices  47.8 us (25%)
  matrix products  45.5 us (23%)
  local copies, waits for them, and re-layouts  32.2 us (17%)
  blocking collectives  8.64 us (4%)
  other arithmetic  6.92 us (4%)
    ppermute x12, waiting for transfers between devices, with_halo(): after = lax.ppermute(initial, axis, down)  42.3 us
    dot_general x36, matrix products, convolve(): jnp.einsum('oid,dixyz->oxyz', taps, slab, preferred_element_type=jnp.floa...  38.4 us
    ppermute x12, starting transfers between devices, with_halo(): before = lax.ppermute(last, axis, up)  33.7 us
    ppermute x12, starting transfers between devices, with_halo(): after = lax.ppermute(initial, axis, down)  16.1 us
    slice x4, local copies, waits for them, and re-layouts, convolve(): slab = shifted[:, :, step_x:step_x + depth, step_y:step_y + height, :]  15 us
    dot_general x4, matrix products, convolve(): jnp.einsum('cxyw,wdz->dcxyz', padded, band_table(width), preferred_elemen...  7.04 us
    concatenate x7, other arithmetic, with_halo(): value = jnp.concatenate([before, value, after], axis=dim)  6.71 us
    ppermute x12, waiting for transfers between devices, with_halo(): before = lax.ppermute(last, axis, up)  5.5 us
  transfers between devices with their start and end apart: 24, of which 17 were waited for; matrix products, arithmetic and copies ran while one was open for 3% of the time, Pallas kernels for 0%

profile of v1, /device:TPU:0, one launch (start us, length us, event | category | flops | bytes accessed | tf_op | source)
XLA Modules:
  0.0 191.6 jit_solution(2719549731387878683)
XLA Ops:
  1.3 4.9 %collective-permute-start = (bf16[16,1,32,128]{3,2,1,0:T(8,128)(2,1)S(1)}, bf16[16,1,32,128]{3,2,1,0:T(8,128)(2,1)S(1)}, u32[]{:S(2)}, u32[]{:S(2)}) collective-permute-start(bf16[16,1,32,128]{3,2,1,0:T(8,128)(2,1)S(1)} %get-tuple-element.63), channel_id=1, source_target_pairs={{0,8},{1,9},{2,10},{3,11},{4,12},{5,13},{6,14},{7,15},{16,24},{17,... | collective-permute-start | bytes 393224 | tf_op jit(solution)/shard_map/ppermute | solution.py:14
  7.5 2.1 %all_gather.6 = bf16[2,2,16,16,3,3,3]{3,2,6,5,4,1,0:T(8,128)(2,1)S(1)} all-gather(bf16[1,2,16,16,3,3,3]{3,2,6,5,4,1,0:T(8,128)(2,1)S(1)} %copy-done.2), channel_id=1, replica_groups=mesh['segment'=2,'gx'=2,'gy'=4,'gz'=2] {'segment'}, dimensions={0}, use_global_device_ids=true | all-gather | bytes 82944 | tf_op jit(solution)/shard_map/all_gather | solution.py:55
  9.6 3.4 %collective-permute-done.1 = bf16[16,1,32,128]{3,2,1,0:T(8,128)(2,1)S(1)} collective-permute-done((bf16[16,1,32,128]{3,2,1,0:T(8,128)(2,1)S(1)}, bf16[16,1,32,128]{3,2,1,0:T(8,128)(2,1)S(1)}, u32[]{:S(2)}, u32[]{:S(2)}) %collective-permute-start.1) | collective-permute-done | bytes 131104 | tf_op jit(solution)/shard_map/ppermute | solution.py:15
  13.1 3.5 %collective-permute-start.2 = (bf16[16,6,1,128]{3,2,1,0:T(2,128)(2,1)S(1)}, bf16[16,6,1,128]{3,2,1,0:T(2,128)(2,1)S(1)}, u32[]{:S(2)}, u32[]{:S(2)}) collective-permute-start(bf16[16,6,1,128]{3,2,1,0:T(2,128)(2,1)S(1)} %get-tuple-element.55), channel_id=1, source_target_pairs={{0,2},{2,4},{4,6},{1,3},{3,5},{5,7},{8,10},{10,12},{12,14},{9,11},... | collective-permute-start | bytes 73736 | tf_op jit(solution)/shard_map/ppermute | solution.py:14
  18.0 1.8 all_gather.7
  19.8 2.8 %collective-permute-done.3 = bf16[16,6,1,128]{3,2,1,0:T(2,128)(2,1)S(1)} collective-permute-done((bf16[16,6,1,128]{3,2,1,0:T(2,128)(2,1)S(1)}, bf16[16,6,1,128]{3,2,1,0:T(2,128)(2,1)S(1)}, u32[]{:S(2)}, u32[]{:S(2)}) %collective-permute-start.3) | collective-permute-done | bytes 24608 | tf_op jit(solution)/shard_map/ppermute | solution.py:15
  26.2 4.5 %collective-permute-start.4 = (bf16[16,6,34,1]{2,0,3,1:T(8,128)(2,1)S(1)}, bf16[16,6,34,1]{2,0,3,1:T(8,128)(2,1)S(1)}, u32[]{:S(2)}, u32[]{:S(2)}) collective-permute-start(bf16[16,6,34,1]{2,0,3,1:T(8,128)(2,1)S(1)} %copy.44), channel_id=1, source_target_pairs={{0,1},{2,3},{4,5},{6,7},{8,9},{10,11},{12,13},{14,15},{16,17},{18,... | collective-permute-start | bytes 19592 | tf_op jit(solution)/shard_map/ppermute | solution.py:14
  33.8 2.9 %convert_bitcast_fusion.3 = bf16[3,16,6,34,128]{4,3,2,1,0:T(8,128)(2,1)S(1)} fusion(bf16[16,6,34,1]{3,2,1,0:T(8,128)(2,1)S(1)} %copy.47, bf16[16,6,1,128]{3,2,1,0:T(2,128)(2,1)S(1)} %collective-permute-done.3, bf16[16,1,32,128]{3,2,1,0:T(8,128)(2,1)S(1)} %collective-permute-done.1, bf16[16,4,32,128]{3,2,1,0:T(8,128)(2,1)S(1)} %dynamic-slice_bitcast_fusion, ...), kind=kOutput, calls=%fused_computation.7 | convolution fusion | flops 333271296 | bytes 3355392 | tf_op jit(solution)/shard_map/cxyw,wdz->dcxyz/dot_general | solution.py:32
  36.7 3.7 %fusion.370 = (bf16[3,16,4,32,128]{4,3,2,1,0:T(8,128)(2,1)S(1)}, bf16[3,16,4,32,128]{4,3,2,1,0:T(8,128)(2,1)S(1)}, bf16[3,16,4,32,128]{4,3,2,1,0:T(8,128)(2,1)S(...) fusion(bf16[3,16,6,34,128]{4,3,2,1,0:T(8,128)(2,1)S(1)} %conver, ...), kind=kLoop, calls=%fused_computation.272 | loop fusion | bytes 28311552 | tf_op jit(solution)/shard_map/slice | solution.py:38
  54.1 4.4 %collective-permute-done.7 = bf16[16,1,32,128]{3,0,2,1:T(8,128)(2,1)S(1)} collective-permute-done((bf16[16,1,32,128]{3,0,2,1:T(8,128)(2,1)S(1)}, bf16[16,1,32,128]{3,0,2,1:T(8,128)(2,1)S(1)}, u32[]{:S(2)}, u32[]{:S(2)}) %collective-permute-start.7) | collective-permute-done | bytes 131104 | tf_op jit(solution)/shard_map/ppermute | solution.py:15
  58.4 3.5 %collective-permute-start.8 = (bf16[16,6,1,128]{3,0,2,1:T(8,128)(2,1)S(1)}, bf16[16,6,1,128]{3,0,2,1:T(8,128)(2,1)S(1)}, u32[]{:S(2)}, u32[]{:S(2)}) collective-permute-start(bf16[16,6,1,128]{3,0,2,1:T(8,128)(2,1)S(1)} %get-tuple-element.53), channel_id=1, source_target_pairs={{0,2},{2,4},{4,6},{1,3},{3,5},{5,7},{8,10},{10,12},{12,14},{9,11},... | collective-permute-start | bytes 73736 | tf_op jit(solution)/shard_map/ppermute | solution.py:14
  61.9 1.5 collective-permute-start.9
  63.5 4.2 %collective-permute-done.9 = bf16[16,6,1,128]{3,0,2,1:T(8,128)(2,1)S(1)} collective-permute-done((bf16[16,6,1,128]{3,0,2,1:T(8,128)(2,1)S(1)}, bf16[16,6,1,128]{3,0,2,1:T(8,128)(2,1)S(1)}, u32[]{:S(2)}, u32[]{:S(2)}) %collective-permute-start.9) | collective-permute-done | bytes 24608 | tf_op jit(solution)/shard_map/ppermute | solution.py:15
  69.1 4.2 %collective-permute-start.10 = (bf16[16,6,34,1]{2,0,3,1:T(8,128)(2,1)S(1)}, bf16[16,6,34,1]{2,0,3,1:T(8,128)(2,1)S(1)}, u32[]{:S(2)}, u32[]{:S(2)}) collective-permute-start(bf16[16,6,34,1]{2,0,3,1:T(8,128)(2,1)S(1)} %copy.57), channel_id=1, source_target_pairs={{0,1},{2,3},{4,5},{6,7},{8,9},{10,11},{12,13},{14,15},{16,17},{18,... | collective-permute-start | bytes 19592 | tf_op jit(solution)/shard_map/ppermute | solution.py:14
  76.3 3.6 %collective-permute-done.11 = bf16[16,6,34,1]{2,0,3,1:T(8,128)(2,1)S(1)} collective-permute-done((bf16[16,6,34,1]{2,0,3,1:T(8,128)(2,1)S(1)}, bf16[16,6,34,1]{2,0,3,1:T(8,128)(2,1)S(1)}, u32[]{:S(2)}, u32[]{:S(2)}) %collective-permute-start.11) | collective-permute-done | bytes 6560 | tf_op jit(solution)/shard_map/ppermute | solution.py:15
  80.7 1.9 pad_maximum_fusion
  84.0 4.1 %fusion.369 = (bf16[3,16,4,32,128]{4,3,2,1,0:T(8,128)(2,1)S(1)}, bf16[3,16,4,32,128]{4,3,2,1,0:T(8,128)(2,1)S(1)}, bf16[3,16,4,32,128]{4,3,2,1,0:T(8,128)(2,1)S(...) fusion(bf16[3,16,6,34,128]{4,3,2,1,0:T(8,128)(2,1)S(1)} %conver, ...), kind=kLoop, calls=%fused_computation.271 | loop fusion | bytes 28311552 | tf_op jit(solution)/shard_map/slice | solution.py:38
  101.7 4.4 %collective-permute-done.13 = bf16[16,1,32,128]{3,0,2,1:T(8,128)(2,1)S(1)} collective-permute-done((bf16[16,1,32,128]{3,0,2,1:T(8,128)(2,1)S(1)}, bf16[16,1,32,128]{3,0,2,1:T(8,128)(2,1)S(1)}, u32[]{:S(2)}, u32[]{:S(2)}) %collective-permute-start.13) | collective-permute-done | bytes 131104 | tf_op jit(solution)/shard_map/ppermute | solution.py:15
  106.1 3.5 %collective-permute-start.14 = (bf16[16,6,1,128]{3,0,2,1:T(8,128)(2,1)S(1)}, bf16[16,6,1,128]{3,0,2,1:T(8,128)(2,1)S(1)}, u32[]{:S(2)}, u32[]{:S(2)}) collective-permute-start(bf16[16,6,1,128]{3,0,2,1:T(8,128)(2,1)S(1)} %get-tuple-element.51), channel_id=1, source_target_pairs={{0,2},{2,4},{4,6},{1,3},{3,5},{5,7},{8,10},{10,12},{12,14},{9,11},... | collective-permute-start | bytes 73736 | tf_op jit(solution)/shard_map/ppermute | solution.py:14
  111.1 4.2 %collective-permute-done.15 = bf16[16,6,1,128]{3,0,2,1:T(8,128)(2,1)S(1)} collective-permute-done((bf16[16,6,1,128]{3,0,2,1:T(8,128)(2,1)S(1)}, bf16[16,6,1,128]{3,0,2,1:T(8,128)(2,1)S(1)}, u32[]{:S(2)}, u32[]{:S(2)}) %collective-permute-start.15) | collective-permute-done | bytes 24608 | tf_op jit(solution)/shard_map/ppermute | solution.py:15
  116.7 1.6 collective-permute-start.16
  121.5 3.4 %collective-permute-done.17 = bf16[16,6,34,1]{2,0,3,1:T(8,128)(2,1)S(1)} collective-permute-done((bf16[16,6,34,1]{2,0,3,1:T(8,128)(2,1)S(1)}, bf16[16,6,34,1]{2,0,3,1:T(8,128)(2,1)S(1)}, u32[]{:S(2)}, u32[]{:S(2)}) %collective-permute-start.17) | collective-permute-done | bytes 6560 | tf_op jit(solution)/shard_map/ppermute | solution.py:15
  125.8 1.9 pad_maximum_fusion.1
  129.0 3.7 %fusion.368 = (bf16[3,16,4,32,128]{4,3,2,1,0:T(8,128)(2,1)S(1)}, bf16[3,16,4,32,128]{4,3,2,1,0:T(8,128)(2,1)S(1)}, bf16[3,16,4,32,128]{4,3,2,1,0:T(8,128)(2,1)S(...) fusion(bf16[3,16,6,34,128]{4,3,2,1,0:T(8,128)(2,1)S(1)} %conver, ...), kind=kLoop, calls=%fused_computation.270 | loop fusion | bytes 28311552 | tf_op jit(solution)/shard_map/slice | solution.py:38
  146.3 4.4 %collective-permute-done.19 = bf16[16,1,32,128]{3,0,2,1:T(8,128)(2,1)S(1)} collective-permute-done((bf16[16,1,32,128]{3,0,2,1:T(8,128)(2,1)S(1)}, bf16[16,1,32,128]{3,0,2,1:T(8,128)(2,1)S(1)}, u32[]{:S(2)}, u32[]{:S(2)}) %collective-permute-start.19) | collective-permute-done | bytes 131104 | tf_op jit(solution)/shard_map/ppermute | solution.py:15
  150.7 1.9 %collective-permute-start.20 = (bf16[16,6,1,128]{3,0,2,1:T(8,128)(2,1)S(1)}, bf16[16,6,1,128]{3,0,2,1:T(8,128)(2,1)S(1)}, u32[]{:S(2)}, u32[]{:S(2)}) collective-permute-start(bf16[16,6,1,128]{3,0,2,1:T(8,128)(2,1)S(1)} %get-tuple-element.49), channel_id=1, source_target_pairs={{0,2},{2,4},{4,6},{1,3},{3,5},{5,7},{8,10},{10,12},{12,14},{9,11},... | collective-permute-start | bytes 73736 | tf_op jit(solution)/shard_map/ppermute | solution.py:14
  154.1 4.2 %collective-permute-done.21 = bf16[16,6,1,128]{3,0,2,1:T(8,128)(2,1)S(1)} collective-permute-done((bf16[16,6,1,128]{3,0,2,1:T(8,128)(2,1)S(1)}, bf16[16,6,1,128]{3,0,2,1:T(8,128)(2,1)S(1)}, u32[]{:S(2)}, u32[]{:S(2)}) %collective-permute-start.21) | collective-permute-done | bytes 24608 | tf_op jit(solution)/shard_map/ppermute | solution.py:15
  159.8 1.6 collective-permute-start.22
  164.6 3.4 %collective-permute-done.23 = bf16[16,6,34,1]{2,0,3,1:T(8,128)(2,1)S(1)} collective-permute-done((bf16[16,6,34,1]{2,0,3,1:T(8,128)(2,1)S(1)}, bf16[16,6,34,1]{2,0,3,1:T(8,128)(2,1)S(1)}, u32[]{:S(2)}, u32[]{:S(2)}) %collective-permute-start.23) | collective-permute-done | bytes 6560 | tf_op jit(solution)/shard_map/ppermute | solution.py:15
  168.8 1.9 pad_maximum_fusion.2
  172.1 3.7 %fusion.367 = (bf16[3,16,4,32,128]{4,3,2,1,0:T(8,128)(2,1)S(1)}, bf16[3,16,4,32,128]{4,3,2,1,0:T(8,128)(2,1)S(1)}, bf16[3,16,4,32,128]{4,3,2,1,0:T(8,128)(2,1)S(...) fusion(bf16[3,16,6,34,128]{4,3,2,1,0:T(8,128)(2,1)S(1)} %conver, ...), kind=kLoop, calls=%fused_computation.269 | loop fusion | bytes 28311552 | tf_op jit(solution)/shard_map/slice | solution.py:38
  185.4 4.7 %all_to_all.5 = bf16[2,1,1,16,4,32,128]{6,3,5,4,2,1,0:T(8,128)(2,1)S(1)} all-to-all(bf16[2,1,1,16,4,32,128]{6,3,5,4,2,1,0:T(8,128)(2,1)S(1)} %pad_maximum_fusion.3), channel_id=1, replica_groups=mesh['segment'=2,'gx'=2,'gy'=4,'gz'=2] {'segment'}, dimensions={0} | all-to-all | bytes 2097152 | tf_op jit(solution)/shard_map/all_to_all | solution.py:66
  (111 shorter events, 85.5 us)
Async XLA Ops:
  0.0 1.2 copy-start
  0.0 7.5 %copy-start.2 = (bf16[1,2,16,16,3,3,3]{3,2,6,5,4,1,0:T(8,128)(2,1)S(1)}, bf16[1,2,16,16,3,3,3]{3,2,6,5,4,1,0:T(8,128)(2,1)}, u32[]{:S(2)}) copy-start(bf16[1,2,16,16,3,3,3]{3,2,6,5,4,1,0:T(8,128)(2,1)} %param.4) | copy-start | bytes 82948
  1.3 16.7 %copy-start.3 = (bf16[1,2,16]{2,1,0:T(2,128)(2,1)S(1)}, bf16[1,2,16]{2,1,0:T(2,128)(2,1)}, u32[]{:S(2)}) copy-start(bf16[1,2,16]{2,1,0:T(2,128)(2,1)} %param.5) | copy-start | bytes 196
  1.3 8.3 %collective-permute-start = (bf16[16,1,32,128]{3,2,1,0:T(8,128)(2,1)S(1)}, bf16[16,1,32,128]{3,2,1,0:T(8,128)(2,1)S(1)}, u32[]{:S(2)}, u32[]{:S(2)}) collective-permute-start(bf16[16,1,32,128]{3,2,1,0:T(8,128)(2,1)S(1)} %get-tuple-element.63), channel_id=1, source_target_pairs={{0,8},{1,9},{2,10},{3,11},{4,12},{5,13},{6,14},{7,15},{16,24},{17,... | collective-permute-start | bytes 393224 | tf_op jit(solution)/shard_map/ppermute | solution.py:14
  6.2 6.9 %collective-permute-start.1 = (bf16[16,1,32,128]{3,2,1,0:T(8,128)(2,1)S(1)}, bf16[16,1,32,128]{3,2,1,0:T(8,128)(2,1)S(1)}, u32[]{:S(2)}, u32[]{:S(2)}) collective-permute-start(bf16[16,1,32,128]{3,2,1,0:T(8,128)(2,1)S(1)} %get-tuple-element.64), channel_id=1, source_target_pairs={{8,0},{9,1},{10,2},{11,3},{12,4},{13,5},{14,6},{15,7},{24,16},{25,... | collective-permute-start | bytes 393224 | tf_op jit(solution)/shard_map/ppermute | solution.py:15
  13.1 6.7 %collective-permute-start.2 = (bf16[16,6,1,128]{3,2,1,0:T(2,128)(2,1)S(1)}, bf16[16,6,1,128]{3,2,1,0:T(2,128)(2,1)S(1)}, u32[]{:S(2)}, u32[]{:S(2)}) collective-permute-start(bf16[16,6,1,128]{3,2,1,0:T(2,128)(2,1)S(1)} %get-tuple-element.55), channel_id=1, source_target_pairs={{0,2},{2,4},{4,6},{1,3},{3,5},{5,7},{8,10},{10,12},{12,14},{9,11},... | collective-permute-start | bytes 73736 | tf_op jit(solution)/shard_map/ppermute | solution.py:14
  16.6 6.0 %collective-permute-start.3 = (bf16[16,6,1,128]{3,2,1,0:T(2,128)(2,1)S(1)}, bf16[16,6,1,128]{3,2,1,0:T(2,128)(2,1)S(1)}, u32[]{:S(2)}, u32[]{:S(2)}) collective-permute-start(bf16[16,6,1,128]{3,2,1,0:T(2,128)(2,1)S(1)} %get-tuple-element.56), channel_id=1, source_target_pairs={{2,0},{4,2},{6,4},{3,1},{5,3},{7,5},{10,8},{12,10},{14,12},{11,9},... | collective-permute-start | bytes 73736 | tf_op jit(solution)/shard_map/ppermute | solution.py:15
  24.9 8.1 %collective-permute-start.5 = (bf16[16,6,34,1]{2,0,3,1:T(8,128)(2,1)S(1)}, bf16[16,6,34,1]{2,0,3,1:T(8,128)(2,1)S(1)}, u32[]{:S(2)}, u32[]{:S(2)}) collective-permute-start(bf16[16,6,34,1]{2,0,3,1:T(8,128)(2,1)S(1)} %copy.45), channel_id=1, source_target_pairs={{1,0},{3,2},{5,4},{7,6},{9,8},{11,10},{13,12},{15,14},{17,16},{19,... | collective-permute-start | bytes 19592 | tf_op jit(solution)/shard_map/ppermute | solution.py:15
  26.2 6.1 %collective-permute-start.4 = (bf16[16,6,34,1]{2,0,3,1:T(8,128)(2,1)S(1)}, bf16[16,6,34,1]{2,0,3,1:T(8,128)(2,1)S(1)}, u32[]{:S(2)}, u32[]{:S(2)}) collective-permute-start(bf16[16,6,34,1]{2,0,3,1:T(8,128)(2,1)S(1)} %copy.44), channel_id=1, source_target_pairs={{0,1},{2,3},{4,5},{6,7},{8,9},{10,11},{12,13},{14,15},{16,17},{18,... | collective-permute-start | bytes 19592 | tf_op jit(solution)/shard_map/ppermute | solution.py:14
  50.1 4.0 %collective-permute-start.6 = (bf16[16,1,32,128]{3,0,2,1:T(8,128)(2,1)S(1)}, bf16[16,1,32,128]{3,0,2,1:T(8,128)(2,1)S(1)}, u32[]{:S(2)}, u32[]{:S(2)}) collective-permute-start(bf16[16,1,32,128]{3,0,2,1:T(8,128)(2,1)S(1)} %get-tuple-element.61), channel_id=1, source_target_pairs={{0,8},{1,9},{2,10},{3,11},{4,12},{5,13},{6,14},{7,15},{16,24},{17,... | collective-permute-start | bytes 393224 | tf_op jit(solution)/shard_map/ppermute | solution.py:14
  51.6 6.9 %collective-permute-start.7 = (bf16[16,1,32,128]{3,0,2,1:T(8,128)(2,1)S(1)}, bf16[16,1,32,128]{3,0,2,1:T(8,128)(2,1)S(1)}, u32[]{:S(2)}, u32[]{:S(2)}) collective-permute-start(bf16[16,1,32,128]{3,0,2,1:T(8,128)(2,1)S(1)} %get-tuple-element.62), channel_id=1, source_target_pairs={{8,0},{9,1},{10,2},{11,3},{12,4},{13,5},{14,6},{15,7},{24,16},{25,... | collective-permute-start | bytes 393224 | tf_op jit(solution)/shard_map/ppermute | solution.py:15
  58.4 5.0 %collective-permute-start.8 = (bf16[16,6,1,128]{3,0,2,1:T(8,128)(2,1)S(1)}, bf16[16,6,1,128]{3,0,2,1:T(8,128)(2,1)S(1)}, u32[]{:S(2)}, u32[]{:S(2)}) collective-permute-start(bf16[16,6,1,128]{3,0,2,1:T(8,128)(2,1)S(1)} %get-tuple-element.53), channel_id=1, source_target_pairs={{0,2},{2,4},{4,6},{1,3},{3,5},{5,7},{8,10},{10,12},{12,14},{9,11},... | collective-permute-start | bytes 73736 | tf_op jit(solution)/shard_map/ppermute | solution.py:14
  61.9 5.7 %collective-permute-start.9 = (bf16[16,6,1,128]{3,0,2,1:T(8,128)(2,1)S(1)}, bf16[16,6,1,128]{3,0,2,1:T(8,128)(2,1)S(1)}, u32[]{:S(2)}, u32[]{:S(2)}) collective-permute-start(bf16[16,6,1,128]{3,0,2,1:T(8,128)(2,1)S(1)} %get-tuple-element.54), channel_id=1, source_target_pairs={{2,0},{4,2},{6,4},{3,1},{5,3},{7,5},{10,8},{12,10},{14,12},{11,9},... | collective-permute-start | bytes 73736 | tf_op jit(solution)/shard_map/ppermute | solution.py:15
  69.1 6.4 %collective-permute-start.10 = (bf16[16,6,34,1]{2,0,3,1:T(8,128)(2,1)S(1)}, bf16[16,6,34,1]{2,0,3,1:T(8,128)(2,1)S(1)}, u32[]{:S(2)}, u32[]{:S(2)}) collective-permute-start(bf16[16,6,34,1]{2,0,3,1:T(8,128)(2,1)S(1)} %copy.57), channel_id=1, source_target_pairs={{0,1},{2,3},{4,5},{6,7},{8,9},{10,11},{12,13},{14,15},{16,17},{18,... | collective-permute-start | bytes 19592 | tf_op jit(solution)/shard_map/ppermute | solution.py:14
  74.2 5.7 %collective-permute-start.11 = (bf16[16,6,34,1]{2,0,3,1:T(8,128)(2,1)S(1)}, bf16[16,6,34,1]{2,0,3,1:T(8,128)(2,1)S(1)}, u32[]{:S(2)}, u32[]{:S(2)}) collective-permute-start(bf16[16,6,34,1]{2,0,3,1:T(8,128)(2,1)S(1)} %copy.58), channel_id=1, source_target_pairs={{1,0},{3,2},{5,4},{7,6},{9,8},{11,10},{13,12},{15,14},{17,16},{19,... | collective-permute-start | bytes 19592 | tf_op jit(solution)/shard_map/ppermute | solution.py:15
  97.7 4.0 %collective-permute-start.12 = (bf16[16,1,32,128]{3,0,2,1:T(8,128)(2,1)S(1)}, bf16[16,1,32,128]{3,0,2,1:T(8,128)(2,1)S(1)}, u32[]{:S(2)}, u32[]{:S(2)}) collective-permute-start(bf16[16,1,32,128]{3,0,2,1:T(8,128)(2,1)S(1)} %get-tuple-element.59), channel_id=1, source_target_pairs={{0,8},{1,9},{2,10},{3,11},{4,12},{5,13},{6,14},{7,15},{16,24},{17,... | collective-permute-start | bytes 393224 | tf_op jit(solution)/shard_map/ppermute | solution.py:14
  99.2 6.9 %collective-permute-start.13 = (bf16[16,1,32,128]{3,0,2,1:T(8,128)(2,1)S(1)}, bf16[16,1,32,128]{3,0,2,1:T(8,128)(2,1)S(1)}, u32[]{:S(2)}, u32[]{:S(2)}) collective-permute-start(bf16[16,1,32,128]{3,0,2,1:T(8,128)(2,1)S(1)} %get-tuple-element.60), channel_id=1, source_target_pairs={{8,0},{9,1},{10,2},{11,3},{12,4},{13,5},{14,6},{15,7},{24,16},{25,... | collective-permute-start | bytes 393224 | tf_op jit(solution)/shard_map/ppermute | solution.py:15
  106.1 5.0 %collective-permute-start.14 = (bf16[16,6,1,128]{3,0,2,1:T(8,128)(2,1)S(1)}, bf16[16,6,1,128]{3,0,2,1:T(8,128)(2,1)S(1)}, u32[]{:S(2)}, u32[]{:S(2)}) collective-permute-start(bf16[16,6,1,128]{3,0,2,1:T(8,128)(2,1)S(1)} %get-tuple-element.51), channel_id=1, source_target_pairs={{0,2},{2,4},{4,6},{1,3},{3,5},{5,7},{8,10},{10,12},{12,14},{9,11},... | collective-permute-start | bytes 73736 | tf_op jit(solution)/shard_map/ppermute | solution.py:14
  109.6 5.7 %collective-permute-start.15 = (bf16[16,6,1,128]{3,0,2,1:T(8,128)(2,1)S(1)}, bf16[16,6,1,128]{3,0,2,1:T(8,128)(2,1)S(1)}, u32[]{:S(2)}, u32[]{:S(2)}) collective-permute-start(bf16[16,6,1,128]{3,0,2,1:T(8,128)(2,1)S(1)} %get-tuple-element.52), channel_id=1, source_target_pairs={{2,0},{4,2},{6,4},{3,1},{5,3},{7,5},{10,8},{12,10},{14,12},{11,9},... | collective-permute-start | bytes 73736 | tf_op jit(solution)/shard_map/ppermute | solution.py:15
  116.7 4.0 %collective-permute-start.16 = (bf16[16,6,34,1]{2,0,3,1:T(8,128)(2,1)S(1)}, bf16[16,6,34,1]{2,0,3,1:T(8,128)(2,1)S(1)}, u32[]{:S(2)}, u32[]{:S(2)}) collective-permute-start(bf16[16,6,34,1]{2,0,3,1:T(8,128)(2,1)S(1)} %copy.71), channel_id=1, source_target_pairs={{0,1},{2,3},{4,5},{6,7},{8,9},{10,11},{12,13},{14,15},{16,17},{18,... | collective-permute-start | bytes 19592 | tf_op jit(solution)/shard_map/ppermute | solution.py:14
  119.2 5.7 %collective-permute-start.17 = (bf16[16,6,34,1]{2,0,3,1:T(8,128)(2,1)S(1)}, bf16[16,6,34,1]{2,0,3,1:T(8,128)(2,1)S(1)}, u32[]{:S(2)}, u32[]{:S(2)}) collective-permute-start(bf16[16,6,34,1]{2,0,3,1:T(8,128)(2,1)S(1)} %copy.72), channel_id=1, source_target_pairs={{1,0},{3,2},{5,4},{7,6},{9,8},{11,10},{13,12},{15,14},{17,16},{19,... | collective-permute-start | bytes 19592 | tf_op jit(solution)/shard_map/ppermute | solution.py:15
  142.3 4.0 %collective-permute-start.18 = (bf16[16,1,32,128]{3,0,2,1:T(8,128)(2,1)S(1)}, bf16[16,1,32,128]{3,0,2,1:T(8,128)(2,1)S(1)}, u32[]{:S(2)}, u32[]{:S(2)}) collective-permute-start(bf16[16,1,32,128]{3,0,2,1:T(8,128)(2,1)S(1)} %get-tuple-element.57), channel_id=1, source_target_pairs={{0,8},{1,9},{2,10},{3,11},{4,12},{5,13},{6,14},{7,15},{16,24},{17,... | collective-permute-start | bytes 393224 | tf_op jit(solution)/shard_map/ppermute | solution.py:14
  143.8 6.9 %collective-permute-start.19 = (bf16[16,1,32,128]{3,0,2,1:T(8,128)(2,1)S(1)}, bf16[16,1,32,128]{3,0,2,1:T(8,128)(2,1)S(1)}, u32[]{:S(2)}, u32[]{:S(2)}) collective-permute-start(bf16[16,1,32,128]{3,0,2,1:T(8,128)(2,1)S(1)} %get-tuple-element.58), channel_id=1, source_target_pairs={{8,0},{9,1},{10,2},{11,3},{12,4},{13,5},{14,6},{15,7},{24,16},{25,... | collective-permute-start | bytes 393224 | tf_op jit(solution)/shard_map/ppermute | solution.py:15
  150.7 3.4 %collective-permute-start.20 = (bf16[16,6,1,128]{3,0,2,1:T(8,128)(2,1)S(1)}, bf16[16,6,1,128]{3,0,2,1:T(8,128)(2,1)S(1)}, u32[]{:S(2)}, u32[]{:S(2)}) collective-permute-start(bf16[16,6,1,128]{3,0,2,1:T(8,128)(2,1)S(1)} %get-tuple-element.49), channel_id=1, source_target_pairs={{0,2},{2,4},{4,6},{1,3},{3,5},{5,7},{8,10},{10,12},{12,14},{9,11},... | collective-permute-start | bytes 73736 | tf_op jit(solution)/shard_map/ppermute | solution.py:14
  152.6 5.7 %collective-permute-start.21 = (bf16[16,6,1,128]{3,0,2,1:T(8,128)(2,1)S(1)}, bf16[16,6,1,128]{3,0,2,1:T(8,128)(2,1)S(1)}, u32[]{:S(2)}, u32[]{:S(2)}) collective-permute-start(bf16[16,6,1,128]{3,0,2,1:T(8,128)(2,1)S(1)} %get-tuple-element.50), channel_id=1, source_target_pairs={{2,0},{4,2},{6,4},{3,1},{5,3},{7,5},{10,8},{12,10},{14,12},{11,9},... | collective-permute-start | bytes 73736 | tf_op jit(solution)/shard_map/ppermute | solution.py:15
  159.8 4.0 %collective-permute-start.22 = (bf16[16,6,34,1]{2,0,3,1:T(8,128)(2,1)S(1)}, bf16[16,6,34,1]{2,0,3,1:T(8,128)(2,1)S(1)}, u32[]{:S(2)}, u32[]{:S(2)}) collective-permute-start(bf16[16,6,34,1]{2,0,3,1:T(8,128)(2,1)S(1)} %copy.85), channel_id=1, source_target_pairs={{0,1},{2,3},{4,5},{6,7},{8,9},{10,11},{12,13},{14,15},{16,17},{18,... | collective-permute-start | bytes 19592 | tf_op jit(solution)/shard_map/ppermute | solution.py:14
  162.2 5.7 %collective-permute-start.23 = (bf16[16,6,34,1]{2,0,3,1:T(8,128)(2,1)S(1)}, bf16[16,6,34,1]{2,0,3,1:T(8,128)(2,1)S(1)}, u32[]{:S(2)}, u32[]{:S(2)}) collective-permute-start(bf16[16,6,34,1]{2,0,3,1:T(8,128)(2,1)S(1)} %copy.86), channel_id=1, source_target_pairs={{1,0},{3,2},{5,4},{7,6},{9,8},{11,10},{13,12},{15,14},{17,16},{19,... | collective-permute-start | bytes 19592 | tf_op jit(solution)/shard_map/ppermute | solution.py:15
  185.4 6.0 %copy-start.1 = (bf16[2,16,4,32,128]{4,3,2,1,0:T(8,128)(2,1)S(1)}, bf16[2,16,4,32,128]{4,3,2,1,0:T(8,128)(2,1)}, u32[]{:S(2)}) copy-start(bf16[2,16,4,32,128]{4,3,2,1,0:T(8,128)(2,1)} %param.3) | copy-start | bytes 3145732
